TPU v7x, 512 devices: a whole 4x4x16 slice. The times are simulated.
512 devices in a mesh: tm: 16 (over y, x_lo, core), chan: 32 (over z, x_hi).
Axes of the slice: x: 4 (x_hi: 2, x_lo: 2; x = x_hi * 2 + x_lo), y: 4, z: 16, core: 2. Of those that a mesh axis runs over, the one named last changes fastest.
Arguments:
- raw: bfloat16 [16384, 4096], P('tm', 'chan'), may hold values from -6 to 6
- taps: bfloat16 [512], replicated, may hold values from -0.25 to 0.25
Outputs:
- correlations: float32 [4096, 64, 1024], P('chan', 'tm')
All inputs are finite; a program needn't handle non-finite values.
Results may differ from a plain program's by a relative error of at most 0.0044.
Values may be sent and summed in bfloat16 or wider, within the bound.
No kernel may reach another device: no remote copies, remote signals or barrier semaphores. Data moves between devices by JAX's collectives and lax.ppermute only.
A program may use at most 128 MiB of HBM per device.

v0:
```python
import math
import jax
import jax.numpy as jnp
from jax import lax
from jax.sharding import PartitionSpec as P

TAPS = 512
HW = 64
FR = 1024
SRC_DEV = 2
LAGS = 1024
epsilon = 1e-05


def shifted(block, axis, distance):
    devices = range(lax.axis_size(axis))
    route = [(i - distance, i) for i in devices if i - distance in devices]
    return lax.ppermute(block, axis, route)


def padded(array, sides, width):
    for axis, dim in sides:
        count, length = (lax.axis_size(axis), array.shape[dim])
        up = [(i, (i + 1) % count) for i in range(count - 1)]
        down = [(j, i) for i, j in up]
        last = lax.slice_in_dim(array, length - width, length, axis=dim)
        initial = lax.slice_in_dim(array, 0, width, axis=dim)
        before = lax.ppermute(last, axis, up)
        after = lax.ppermute(initial, axis, down)
        array = jnp.concatenate([before, array, after], axis=dim)
    return array


def forward_table(first, count):
    freq = first + jnp.arange(count, dtype=jnp.int32)
    sample = jnp.arange(FR, dtype=jnp.int32)
    phase = freq[:, None] * sample[None, :] % (2 * FR)
    angle = phase.astype(jnp.float32) * (math.pi / FR)
    return jnp.stack([jnp.cos(angle), -jnp.sin(angle)])


def inverse_table(first, count, scale):
    freq = first + jnp.arange(count, dtype=jnp.int32)
    lagged = jnp.arange(LAGS, dtype=jnp.int32) - LAGS // 2 + 2 * FR
    phase = freq[:, None] * lagged[None, :] % (2 * FR)
    angle = phase.astype(jnp.float32) * (math.pi / FR)
    weight = jnp.where(freq == 0, 1.0, 2.0).astype(jnp.float32) * (scale / (2 * FR))
    return jnp.stack([weight[:, None] * jnp.cos(angle), -weight[:, None] * jnp.sin(angle)])


def transform(frames32, pattern, axis_out):
    width = min(256, FR)
    pieces = []
    for first in range(0, FR, width):
        table = forward_table(first, width)
        pieces.append(jnp.einsum(pattern, table, frames32, precision=lax.Precision.HIGHEST))
    return jnp.concatenate(pieces, axis_out)


def correlate(cross, scale):
    width = min(256, FR)
    result = jnp.zeros(cross.shape[:2] + (LAGS,), jnp.float32)
    for first in range(0, FR, width):
        table = inverse_table(first, width, scale)
        result = result + jnp.einsum(
            "rkgf,gfl->rkl",
            cross[..., first : first + width],
            table,
            precision=lax.Precision.HIGHEST,
        )
    return result


def on_device(raw, taps):
    samples, channels = raw.shape
    time_parts = lax.axis_size("tm")
    chan_parts = lax.axis_size("chan")
    frames_dev = samples // FR
    frame_total = frames_dev * time_parts
    sources_total = SRC_DEV * chan_parts
    stride = channels // SRC_DEV
    scale = 1.0 / math.sqrt(frame_total * FR)
    kernel = jnp.broadcast_to(taps[:, None, None], (TAPS, 1, channels))
    before = shifted(raw[samples - TAPS + 1 :], "tm", 1)
    filtered = lax.conv_general_dilated(
        jnp.concatenate([before, raw], 0)[None],
        kernel,
        (1,),
        "VALID",
        dimension_numbers=("NWC", "WIO", "NWC"),
        feature_group_count=channels,
        preferred_element_type=jnp.float32,
    )[0]
    widened = padded(filtered, (("tm", 0),), HW)
    total = lax.reduce_window(
        jnp.abs(widened), jnp.zeros((), jnp.float32), lax.add, (2 * HW + 1, 1), (1, 1), "VALID"
    )
    level = total / (2 * HW + 1)
    whitened = (widened[HW : HW + samples] / (level + epsilon)).astype(jnp.bfloat16)
    frames32 = whitened.astype(jnp.float32).reshape(frames_dev, FR, channels)
    spectra = transform(frames32, "gft,btc->bgfc", 2).astype(jnp.bfloat16)
    banded = lax.all_to_all(spectra, "tm", split_axis=2, concat_axis=0, tiled=True)
    own_re = banded[:, 0]
    own_im = banded[:, 1]
    picked = banded[..., ::stride]
    band_width = banded.shape[2]
    empty = jnp.zeros((channels, sources_total, 2, band_width), jnp.float32)
    piece = lax.all_gather(picked, "chan", axis=3, tiled=True)
    piece_re = piece[:, 0]
    piece_im = piece[:, 1]
    real_part = jnp.einsum(
        "bfs,bfc->csf", piece_re, own_re, preferred_element_type=jnp.float32
    ) + jnp.einsum("bfs,bfc->csf", piece_im, own_im, preferred_element_type=jnp.float32)
    imag_part = jnp.einsum(
        "bfs,bfc->csf", piece_re, own_im, preferred_element_type=jnp.float32
    ) - jnp.einsum("bfs,bfc->csf", piece_im, own_re, preferred_element_type=jnp.float32)
    stacked = jnp.stack([real_part, imag_part], 2)
    cross = lax.dynamic_update_slice_in_dim(empty, stacked, jnp.int32(0), 1)
    return correlate(lax.all_to_all(cross, "tm", split_axis=1, concat_axis=3, tiled=True), scale)


def solution(mesh):
    placed = (P("tm", "chan"), P())
    return jax.shard_map(
        on_device, mesh=mesh, in_specs=placed, out_specs=P("chan", "tm", None), check_vma=False
    )
```

profile of v0, /device:TPU:1, one launch (start us, length us, event | category | flops | bytes accessed | tf_op | source)
XLA Modules:
  0.0 304.3 jit_solution(13636452753575318065)
XLA Ops:
  0.0 1.0 slice.42
  1.0 4.5 %collective-permute-start = (bf16[511,128]{1,0:T(8,128)(2,1)S(1)}, bf16[511,128]{1,0:T(8,128)(2,1)S(1)}, u32[]{:S(2)}, u32[]{:S(2)}) collective-permute-start(bf16[511,128]{1,0:T(8,128)(2,1)S(1)} %slice.42), channel_id=1, source_target_pairs={{0,32},{32,64},{64,96},{96,128},{128,160},{160,192},{192,224},{224... | collective-permute-start | bytes 392456 | tf_op jit(solution)/shard_map/ppermute | solution.py:18
  5.6 32.5 %cosine_multiply_fusion = (f32[1,256,1024]{2,1,0:T(8,128)}, f32[1,256,1024]{2,1,0:T(8,128)}, f32[1,256,1024]{2,1,0:T(8,128)}, f32[1,256,1024]{2,1,0:T(8,128)}, f...) fusion(f32[256]{0:T(256)S(1)} %get-tuple-element.30, ...), kind=kLoop, calls=%fused_computation.105 | loop fusion | flops 28573696 | bytes 14695424 | tf_op jit(solution)/shard_map/mul | solution.py:48
  38.1 0.6 fusion.132
  38.8 44.4 %fusion.95 = f32[1,1024,128]{2,0,1:T(1,128)S(1)} fusion(bf16[1,1535,128]{2,1,0:T(8,128)(2,1)S(1)} %maximum_bitcast_fusion.10, bf16[512,1,128]{2,1,0:T(2,128)(2,1)S(1)} %fusion.132), kind=kOutput, calls=%fused_computation.131 | convolution fusion | flops 134217728 | bytes 1048320 | tf_op jit(solution)/shard_map/conv_general_dilated | solution.py:85
  83.2 1.9 collective-permute-start.1
  85.1 4.9 %collective-permute-start.2 = (f32[64,128]{1,0:T(8,128)S(1)}, f32[64,128]{1,0:T(8,128)S(1)}, u32[]{:S(2)}, u32[]{:S(2)}) collective-permute-start(f32[64,128]{1,0:T(8,128)S(1)} %get-tuple-element.8), channel_id=1, source_target_pairs={{32,0},{64,32},{96,64},{128,96},{160,128},{192,160},{224,192},{256... | collective-permute-start | bytes 98312 | tf_op jit(solution)/shard_map/ppermute | solution.py:29
  90.1 4.1 %sine_negate_fusion.3 = (f32[1,256,1024]{2,1,0:T(8,128)S(1)}, f32[1,256,1024]{2,1,0:T(8,128)S(1)}) fusion(), kind=kLoop, calls=%fused_computation.123 | loop fusion | flops 3932160 | bytes 2097152 | tf_op jit(solution)/shard_map/neg | solution.py:39
  94.2 0.9 maximum_abs_fusion
  95.2 19.6 %reduce_window.7 = f32[1,1024,128]{2,1,0:T(8,128)} reduce-window(f32[1,1152,128]{2,1,0:T(8,128)} %maximum_abs_fusion, f32[]{:T(128)} %constant.65.clone.1), window={size=1x129x1}, to_apply=%region_0.0 | reduce-window | flops 16777216 | bytes 1114116 | tf_op jit(solution)/shard_map/reduce_window | solution.py:95
  114.8 1.4 divide_convert_fusion
  116.2 1.7 fusion.40
  118.0 1.3 fusion.46
  119.3 1.3 fusion.43
  120.6 1.3 fusion.49
  122.4 12.6 %all_to_all.36 = bf16[1,2,1024,128]{3,1,0,2:T(2,128)(2,1)S(1)} all-to-all(bf16[1,2,1024,128]{3,1,0,2:T(2,128)(2,1)S(1)} %copy.91), channel_id=1, replica_groups=mesh['tm'=16,'chan'=32] {'tm'}, dimensions={2} | all-to-all | bytes 1048576 | tf_op jit(solution)/shard_map/all_to_all | solution.py:102
  135.4 2.0 slice.48
  137.4 0.5 copy.94
  137.9 71.7 %all_gather.3 = bf16[16,2,64,64]{2,0,1,3:T(8,128)(2,1)S(1)} all-gather(bf16[16,2,64,2]{2,0,1,3:T(8,128)(2,1)S(1)} %copy.94), channel_id=1, replica_groups=mesh['tm'=16,'chan'=32] {'chan'}, dimensions={3}, use_global_device_ids=true | all-gather | bytes 270336 | tf_op jit(solution)/shard_map/all_gather | solution.py:108
  210.1 1.8 fusion.107
  212.8 2.1 subtract_bitcast_fusion
  214.9 0.5 add_bitcast_fusion
  215.4 0.6 pad_maximum_fusion
  215.9 2.4 copy.97
  218.4 66.6 %all_to_all.37 = f32[128,64,2,64]{0,3,2,1:T(8,128)S(1)} all-to-all(f32[128,64,2,64]{0,3,2,1:T(8,128)S(1)} %copy.97), channel_id=1, replica_groups=mesh['tm'=16,'chan'=32] {'tm'}, dimensions={1} | all-to-all | bytes 8388608 | tf_op jit(solution)/shard_map/all_to_all | solution.py:119
  285.0 0.6 copy.98
  285.6 0.6 copy-done.5
  286.6 3.5 %fusion.22 = f32[128,4,1024,1]{2,0,3,1:T(8,128)S(1)} fusion(f32[1,256,1024]{2,1,0:T(8,128)S(1)} %copy-done.5, f32[1,256,1024]{2,1,0:T(8,128)S(1)} %copy-done.6, f32[128,4,2,1024]{0,3,2,1:T(8,128)S(1)} %bitcast.109), kind=kOutput, calls=%fused_computation.26 | convolution fusion | flops 3221749760 | bytes 5242880 | tf_op jit(solution)/shard_map/rkgf,gfl->rkl/dot_general | solution.py:65
  290.2 3.6 %fusion.19 = f32[128,4,1024,1]{2,0,3,1:T(8,128)S(1)} fusion(f32[1,256,1024]{2,1,0:T(8,128)S(1)} %copy-done.3, f32[1,256,1024]{2,1,0:T(8,128)S(1)} %copy-done.4, f32[128,4,2,1024]{0,3,2,1:T(8,128)S(1)} %bitcast.110), kind=kOutput, calls=%fused_computation.22 | convolution fusion | flops 3221749760 | bytes 5242880 | tf_op jit(solution)/shard_map/rkgf,gfl->rkl/dot_general | solution.py:65
  293.8 3.6 %fusion.16 = f32[128,4,1024,1]{2,0,3,1:T(8,128)S(1)} fusion(f32[1,256,1024]{2,1,0:T(8,128)S(1)} %copy-done.1, f32[1,256,1024]{2,1,0:T(8,128)S(1)} %copy-done.2, f32[128,4,2,1024]{0,3,2,1:T(8,128)S(1)} %bitcast.111), kind=kOutput, calls=%fused_computation.18 | convolution fusion | flops 3221749760 | bytes 5242880 | tf_op jit(solution)/shard_map/rkgf,gfl->rkl/dot_general | solution.py:65
  297.3 4.1 %bitcast_add_fusion = f32[128,4,1024]{2,0,1:T(8,128)S(1)} fusion(f32[128,4,1024,1]{2,0,3,1:T(8,128)S(1)} %fusion.22, f32[128,4,1024,1]{2,0,3,1:T(8,128)S(1)} %fusion.19, f32[128,4,1024,1]{2,0,3,1:T(8,128)S(1)} %fusion.16, f32[1,256,1024]{2,1,0:T(8,128)S(1)} %copy-done.13, f32[1,256,1024]{2,1,0:T(8,128)S(1)} %copy-done.12, f32[128,4,2,1024]{0,3,2,1:T(8,128)S(1)} %bitcast.112), kind=kOutput, calls=%fused_computation.33 | convolution fusion | flops 3223322624 | bytes 11534336 | tf_op jit(solution)/shard_map/rkgf,gfl->rkl/dot_general | solution.py:65
  301.4 2.7 copy.103
  (50 shorter events, 2.6 us)
Async XLA Ops:
  0.0 38.1 %copy-start = (bf16[512]{0:T(512)(128)(2,1)S(1)}, bf16[512]{0:T(512)(128)(2,1)}, u32[]{:S(2)}) copy-start(bf16[512]{0:T(512)(128)(2,1)} %param.3) | copy-start | bytes 3076
  1.0 37.7 %collective-permute-start = (bf16[511,128]{1,0:T(8,128)(2,1)S(1)}, bf16[511,128]{1,0:T(8,128)(2,1)S(1)}, u32[]{:S(2)}, u32[]{:S(2)}) collective-permute-start(bf16[511,128]{1,0:T(8,128)(2,1)S(1)} %slice.42), channel_id=1, source_target_pairs={{0,32},{32,64},{64,96},{96,128},{128,160},{160,192},{192,224},{224... | collective-permute-start | bytes 392456 | tf_op jit(solution)/shard_map/ppermute | solution.py:18
  5.6 33.1 %copy-start.15 = (bf16[1024,128]{1,0:T(8,128)(2,1)S(1)}, bf16[1024,128]{1,0:T(8,128)(2,1)}, u32[]{:S(2)}) copy-start(bf16[1024,128]{1,0:T(8,128)(2,1)} %param.2) | copy-start | bytes 786436
  83.2 11.0 %copy-start.14 = (f32[1,1024,128]{2,0,1:T(1,128)}, f32[1,1024,128]{2,0,1:T(1,128)S(1)}, u32[]{:S(2)}) copy-start(f32[1,1024,128]{2,0,1:T(1,128)S(1)} %fusion.95) | copy-start | bytes 1572868
  83.2 11.0 %collective-permute-start.1 = (f32[64,128]{1,0:T(8,128)S(1)}, f32[64,128]{1,0:T(8,128)S(1)}, u32[]{:S(2)}, u32[]{:S(2)}) collective-permute-start(f32[64,128]{1,0:T(8,128)S(1)} %get-tuple-element.7), channel_id=1, source_target_pairs={{0,32},{32,64},{64,96},{96,128},{128,160},{160,192},{192,224},{224... | collective-permute-start | bytes 98312 | tf_op jit(solution)/shard_map/ppermute | solution.py:28
  85.1 9.1 %collective-permute-start.2 = (f32[64,128]{1,0:T(8,128)S(1)}, f32[64,128]{1,0:T(8,128)S(1)}, u32[]{:S(2)}, u32[]{:S(2)}) collective-permute-start(f32[64,128]{1,0:T(8,128)S(1)} %get-tuple-element.8), channel_id=1, source_target_pairs={{32,0},{64,32},{96,64},{128,96},{160,128},{192,160},{224,192},{256... | collective-permute-start | bytes 98312 | tf_op jit(solution)/shard_map/ppermute | solution.py:29
  114.8 3.2 %copy-start.10 = (f32[1,256,1024]{2,1,0:T(8,128)S(1)}, f32[1,256,1024]{2,1,0:T(8,128)}, u32[]{:S(2)}) copy-start(f32[1,256,1024]{2,1,0:T(8,128)} %get-tuple-element.21) | copy-start | bytes 3145732
  114.8 3.2 %copy-start.11 = (f32[1,256,1024]{2,1,0:T(8,128)S(1)}, f32[1,256,1024]{2,1,0:T(8,128)}, u32[]{:S(2)}) copy-start(f32[1,256,1024]{2,1,0:T(8,128)} %get-tuple-element.22) | copy-start | bytes 3145732
  116.2 3.1 %copy-start.8 = (f32[1,256,1024]{2,1,0:T(8,128)S(1)}, f32[1,256,1024]{2,1,0:T(8,128)}, u32[]{:S(2)}) copy-start(f32[1,256,1024]{2,1,0:T(8,128)} %get-tuple-element.23) | copy-start | bytes 3145732
  116.2 3.1 %copy-start.9 = (f32[1,256,1024]{2,1,0:T(8,128)S(1)}, f32[1,256,1024]{2,1,0:T(8,128)}, u32[]{:S(2)}) copy-start(f32[1,256,1024]{2,1,0:T(8,128)} %get-tuple-element.24) | copy-start | bytes 3145732
  118.0 2.7 copy-start.7
  285.0 1.2 copy-start.5
  285.0 1.5 copy-start.6
  286.6 3.6 %copy-start.3 = (f32[1,256,1024]{2,1,0:T(8,128)S(1)}, f32[1,256,1024]{2,1,0:T(8,128)}, u32[]{:S(2)}) copy-start(f32[1,256,1024]{2,1,0:T(8,128)} %get-tuple-element.16) | copy-start | bytes 3145732
  286.6 3.6 %copy-start.4 = (f32[1,256,1024]{2,1,0:T(8,128)S(1)}, f32[1,256,1024]{2,1,0:T(8,128)}, u32[]{:S(2)}) copy-start(f32[1,256,1024]{2,1,0:T(8,128)} %get-tuple-element.17) | copy-start | bytes 3145732
  290.1 3.6 %copy-start.1 = (f32[1,256,1024]{2,1,0:T(8,128)S(1)}, f32[1,256,1024]{2,1,0:T(8,128)}, u32[]{:S(2)}) copy-start(f32[1,256,1024]{2,1,0:T(8,128)} %get-tuple-element.15) | copy-start | bytes 3145732
  290.1 3.6 %copy-start.2 = (f32[1,256,1024]{2,1,0:T(8,128)S(1)}, f32[1,256,1024]{2,1,0:T(8,128)}, u32[]{:S(2)}) copy-start(f32[1,256,1024]{2,1,0:T(8,128)} %get-tuple-element.20) | copy-start | bytes 3145732
  293.7 3.6 %copy-start.12 = (f32[1,256,1024]{2,1,0:T(8,128)S(1)}, f32[1,256,1024]{2,1,0:T(8,128)}, u32[]{:S(2)}) copy-start(f32[1,256,1024]{2,1,0:T(8,128)} %get-tuple-element.9) | copy-start | bytes 3145732
  293.7 3.6 %copy-start.13 = (f32[1,256,1024]{2,1,0:T(8,128)S(1)}, f32[1,256,1024]{2,1,0:T(8,128)}, u32[]{:S(2)}) copy-start(f32[1,256,1024]{2,1,0:T(8,128)} %get-tuple-element.10) | copy-start | bytes 3145732
where the time goes:
time: 307 us; the launch traced here: 304 us
  blocking collectives  151 us (49%)
  matrix products  69.7 us (23%)
  other arithmetic  59.3 us (19%)
  local copies, waits for them, and re-layouts  12.3 us (4%)
  starting transfers between devices  11.4 us (4%)
    all_gather x1, blocking collectives, on_device(): piece = lax.all_gather(picked, 'chan', axis=3, tiled=True)  71.7 us
    all_to_all x1, blocking collectives, on_device(): lax.all_to_all(cross, 'tm', split_axis=1, concat_axis=3, tiled=True)  66.6 us
    conv_general_dilated x1, matrix products, on_device(): lax.conv_general_dilated(jnp.concatenate([before, raw], 0)[None], kernel,...  44.4 us
    mul x1, other arithmetic, inverse_table(): weight[:, None] * jnp.cos(angle)  32.5 us
    another operation x1, other arithmetic, on_device(): lax.reduce_window(jnp.abs(widened), jnp.zeros((), jnp.float32), lax.add,...  19.6 us
    dot_general x4, matrix products, correlate(): jnp.einsum('rkgf,gfl->rkl', cross[..., first:first + width], table, preci...  14.8 us
    all_to_all x1, blocking collectives, on_device(): lax.all_to_all(spectra, 'tm', split_axis=2, concat_axis=0, tiled=True)  12.6 us
  transfers between devices with their start and end apart: 3, of which 0 were waited for; matrix products, arithmetic and copies ran while one was open for 12% of the time, Pallas kernels for 0%

commit v1 on v0

--- a/solution.py
+++ b/solution.py
@@ -105,7 +105,9 @@
     picked = banded[..., ::stride]
     band_width = banded.shape[2]
     empty = jnp.zeros((channels, sources_total, 2, band_width), jnp.float32)
-    piece = lax.all_gather(picked, "chan", axis=3, tiled=True)
+    piece = jnp.concatenate(
+        lax.all_to_all(jnp.stack([picked] * lax.axis_size("chan")), "chan", 0, 0), axis=3
+    )
     piece_re = piece[:, 0]
     piece_im = piece[:, 1]
     real_part = jnp.einsum(

time: 307 us -> 262 us (0.85)
  blocking collectives: 151 us -> 105 us
    all_gather x1 -> x0, blocking collectives: 71.7 us -> none  [on_device(): piece = lax.all_gather(picked, 'chan', axis=3, tiled=True)]
    all_to_all x0 -> x1, blocking collectives: none -> 37.1 us  [on_device(): lax.all_to_all(jnp.stack([picked] * lax.axis_size('chan')), 'chan', 0, 0)]
    all_to_all x1, blocking collectives: 66.6 us -> 54.9 us  [on_device(): lax.all_to_all(cross, 'tm', split_axis=1, concat_axis=3, tiled=True)]
  transfers between devices with their start and end apart: 3 -> 3, of which waited for: 0 -> 0; matrix products, arithmetic and copies ran while one was open for 12% -> 14% of each run, Pallas kernels for 0% -> 0%
where the time goes in v1:
time: 262 us; the launch traced here: 259 us
  blocking collectives  105 us (40%)
  matrix products  69.7 us (27%)
  other arithmetic  59.3 us (23%)
  local copies, waits for them, and re-layouts  13.2 us (5%)
  starting transfers between devices  11.4 us (4%)
    all_to_all x1, blocking collectives, on_device(): lax.all_to_all(cross, 'tm', split_axis=1, concat_axis=3, tiled=True)  54.9 us
    conv_general_dilated x1, matrix products, on_device(): lax.conv_general_dilated(jnp.concatenate([before, raw], 0)[None], kernel,...  44.4 us
    all_to_all x1, blocking collectives, on_device(): lax.all_to_all(jnp.stack([picked] * lax.axis_size('chan')), 'chan', 0, 0)  37.1 us
    mul x1, other arithmetic, inverse_table(): weight[:, None] * jnp.cos(angle)  32.5 us
    another operation x1, other arithmetic, on_device(): lax.reduce_window(jnp.abs(widened), jnp.zeros((), jnp.float32), lax.add,...  19.6 us
    dot_general x4, matrix products, correlate(): jnp.einsum('rkgf,gfl->rkl', cross[..., first:first + width], table, preci...  14.8 us
    all_to_all x1, blocking collectives, on_device(): lax.all_to_all(spectra, 'tm', split_axis=2, concat_axis=0, tiled=True)  12.6 us
    dot_general x4, matrix products, transform(): jnp.einsum(pattern, table, frames32, precision=lax.Precision.HIGHEST)  5.64 us
  transfers between devices with their start and end apart: 3, of which 0 were waited for; matrix products, arithmetic and copies ran while one was open for 14% of the time, Pallas kernels for 0%

profile of v1, /device:TPU:1, one launch (start us, length us, event | category | flops | bytes accessed | tf_op | source)
XLA Modules:
  0.0 258.9 jit_solution(16370361623956535040)
XLA Ops:
  0.0 1.0 slice.42
  1.0 4.5 %collective-permute-start = (bf16[511,128]{1,0:T(8,128)(2,1)S(1)}, bf16[511,128]{1,0:T(8,128)(2,1)S(1)}, u32[]{:S(2)}, u32[]{:S(2)}) collective-permute-start(bf16[511,128]{1,0:T(8,128)(2,1)S(1)} %slice.42), channel_id=1, source_target_pairs={{0,32},{32,64},{64,96},{96,128},{128,160},{160,192},{192,224},{224... | collective-permute-start | bytes 392456 | tf_op jit(solution)/shard_map/ppermute | solution.py:18
  5.6 32.5 %cosine_multiply_fusion = (f32[1,256,1024]{2,1,0:T(8,128)}, f32[1,256,1024]{2,1,0:T(8,128)}, f32[1,256,1024]{2,1,0:T(8,128)}, f32[1,256,1024]{2,1,0:T(8,128)}, f...) fusion(f32[256]{0:T(256)S(1)} %get-tuple-element.30, ...), kind=kLoop, calls=%fused_computation.105 | loop fusion | flops 28573696 | bytes 14695424 | tf_op jit(solution)/shard_map/mul | solution.py:48
  38.1 0.6 fusion.132
  38.8 44.4 %fusion.95 = f32[1,1024,128]{2,0,1:T(1,128)S(1)} fusion(bf16[1,1535,128]{2,1,0:T(8,128)(2,1)S(1)} %maximum_bitcast_fusion.10, bf16[512,1,128]{2,1,0:T(2,128)(2,1)S(1)} %fusion.132), kind=kOutput, calls=%fused_computation.131 | convolution fusion | flops 134217728 | bytes 1048320 | tf_op jit(solution)/shard_map/conv_general_dilated | solution.py:85
  83.2 1.9 collective-permute-start.1
  85.1 4.9 %collective-permute-start.2 = (f32[64,128]{1,0:T(8,128)S(1)}, f32[64,128]{1,0:T(8,128)S(1)}, u32[]{:S(2)}, u32[]{:S(2)}) collective-permute-start(f32[64,128]{1,0:T(8,128)S(1)} %get-tuple-element.8), channel_id=1, source_target_pairs={{32,0},{64,32},{96,64},{128,96},{160,128},{192,160},{224,192},{256... | collective-permute-start | bytes 98312 | tf_op jit(solution)/shard_map/ppermute | solution.py:29
  90.1 4.1 %sine_negate_fusion.3 = (f32[1,256,1024]{2,1,0:T(8,128)S(1)}, f32[1,256,1024]{2,1,0:T(8,128)S(1)}) fusion(), kind=kLoop, calls=%fused_computation.123 | loop fusion | flops 3932160 | bytes 2097152 | tf_op jit(solution)/shard_map/neg | solution.py:39
  94.2 0.9 maximum_abs_fusion
  95.2 19.6 %reduce_window.7 = f32[1,1024,128]{2,1,0:T(8,128)} reduce-window(f32[1,1152,128]{2,1,0:T(8,128)} %maximum_abs_fusion, f32[]{:T(128)} %constant.65.clone.1), window={size=1x129x1}, to_apply=%region_0.0 | reduce-window | flops 16777216 | bytes 1114116 | tf_op jit(solution)/shard_map/reduce_window | solution.py:95
  114.8 1.4 divide_convert_fusion
  116.2 1.7 fusion.40
  118.0 1.3 fusion.46
  119.3 1.3 fusion.43
  120.6 1.3 fusion.49
  122.4 12.6 %all_to_all.41 = bf16[1,2,1024,128]{3,1,0,2:T(2,128)(2,1)S(1)} all-to-all(bf16[1,2,1024,128]{3,1,0,2:T(2,128)(2,1)S(1)} %copy.96), channel_id=1, replica_groups=mesh['tm'=16,'chan'=32] {'tm'}, dimensions={2} | all-to-all | bytes 1048576 | tf_op jit(solution)/shard_map/all_to_all | solution.py:102
  135.4 2.0 slice.48
  137.4 0.5 copy.99
  138.4 37.1 %all_to_all.42 = bf16[32,2,2048]{2,1,0:T(2,128)(2,1)S(1)} all-to-all(bf16[32,2,2048]{2,1,0:T(2,128)(2,1)S(1)} %reshape.1217), channel_id=1, replica_groups=mesh['tm'=16,'chan'=32] {'chan'}, dimensions={0} | all-to-all | bytes 524288 | tf_op jit(solution)/shard_map/all_to_all | solution.py:109
  176.4 1.8 fusion.107
  179.1 2.1 subtract_bitcast_fusion
  181.2 0.5 add_bitcast_fusion
  181.7 0.6 pad_maximum_fusion
  182.2 2.4 copy.103
  184.7 54.9 %all_to_all.43 = f32[128,64,2,64]{0,3,2,1:T(8,128)S(1)} all-to-all(f32[128,64,2,64]{0,3,2,1:T(8,128)S(1)} %copy.103), channel_id=1, replica_groups=mesh['tm'=16,'chan'=32] {'tm'}, dimensions={1} | all-to-all | bytes 8388608 | tf_op jit(solution)/shard_map/all_to_all | solution.py:121
  239.5 0.6 copy.104
  240.1 0.6 copy-done.5
  241.1 3.5 %fusion.22 = f32[128,4,1024,1]{2,0,3,1:T(8,128)S(1)} fusion(f32[1,256,1024]{2,1,0:T(8,128)S(1)} %copy-done.5, f32[1,256,1024]{2,1,0:T(8,128)S(1)} %copy-done.6, f32[128,4,2,1024]{0,3,2,1:T(8,128)S(1)} %bitcast.115), kind=kOutput, calls=%fused_computation.26 | convolution fusion | flops 3221749760 | bytes 5242880 | tf_op jit(solution)/shard_map/rkgf,gfl->rkl/dot_general | solution.py:65
  244.7 3.6 %fusion.19 = f32[128,4,1024,1]{2,0,3,1:T(8,128)S(1)} fusion(f32[1,256,1024]{2,1,0:T(8,128)S(1)} %copy-done.3, f32[1,256,1024]{2,1,0:T(8,128)S(1)} %copy-done.4, f32[128,4,2,1024]{0,3,2,1:T(8,128)S(1)} %bitcast.116), kind=kOutput, calls=%fused_computation.22 | convolution fusion | flops 3221749760 | bytes 5242880 | tf_op jit(solution)/shard_map/rkgf,gfl->rkl/dot_general | solution.py:65
  248.3 3.6 %fusion.16 = f32[128,4,1024,1]{2,0,3,1:T(8,128)S(1)} fusion(f32[1,256,1024]{2,1,0:T(8,128)S(1)} %copy-done.1, f32[1,256,1024]{2,1,0:T(8,128)S(1)} %copy-done.2, f32[128,4,2,1024]{0,3,2,1:T(8,128)S(1)} %bitcast.117), kind=kOutput, calls=%fused_computation.18 | convolution fusion | flops 3221749760 | bytes 5242880 | tf_op jit(solution)/shard_map/rkgf,gfl->rkl/dot_general | solution.py:65
  251.9 4.1 %bitcast_add_fusion = f32[128,4,1024]{2,0,1:T(8,128)S(1)} fusion(f32[128,4,1024,1]{2,0,3,1:T(8,128)S(1)} %fusion.22, f32[128,4,1024,1]{2,0,3,1:T(8,128)S(1)} %fusion.19, f32[128,4,1024,1]{2,0,3,1:T(8,128)S(1)} %fusion.16, f32[1,256,1024]{2,1,0:T(8,128)S(1)} %copy-done.13, f32[1,256,1024]{2,1,0:T(8,128)S(1)} %copy-done.12, f32[128,4,2,1024]{0,3,2,1:T(8,128)S(1)} %bitcast.118), kind=kOutput, calls=%fused_computation.33 | convolution fusion | flops 3223322624 | bytes 11534336 | tf_op jit(solution)/shard_map/rkgf,gfl->rkl/dot_general | solution.py:65
  256.0 2.7 %copy.109 = f32[128,4,1024]{2,1,0:T(4,128)} copy(f32[128,4,1024]{2,0,1:T(8,128)S(1)} %bitcast_add_fusion) | data formatting | bytes 4194304 | tf_op jit(solution)/shard_map/add | solution.py:65
  (54 shorter events, 3.5 us)
Async XLA Ops:
  0.0 38.1 %copy-start = (bf16[512]{0:T(512)(128)(2,1)S(1)}, bf16[512]{0:T(512)(128)(2,1)}, u32[]{:S(2)}) copy-start(bf16[512]{0:T(512)(128)(2,1)} %param.3) | copy-start | bytes 3076
  1.0 37.7 %collective-permute-start = (bf16[511,128]{1,0:T(8,128)(2,1)S(1)}, bf16[511,128]{1,0:T(8,128)(2,1)S(1)}, u32[]{:S(2)}, u32[]{:S(2)}) collective-permute-start(bf16[511,128]{1,0:T(8,128)(2,1)S(1)} %slice.42), channel_id=1, source_target_pairs={{0,32},{32,64},{64,96},{96,128},{128,160},{160,192},{192,224},{224... | collective-permute-start | bytes 392456 | tf_op jit(solution)/shard_map/ppermute | solution.py:18
  5.6 33.1 %copy-start.15 = (bf16[1024,128]{1,0:T(8,128)(2,1)S(1)}, bf16[1024,128]{1,0:T(8,128)(2,1)}, u32[]{:S(2)}) copy-start(bf16[1024,128]{1,0:T(8,128)(2,1)} %param.2) | copy-start | bytes 786436
  83.2 11.0 %copy-start.14 = (f32[1,1024,128]{2,0,1:T(1,128)}, f32[1,1024,128]{2,0,1:T(1,128)S(1)}, u32[]{:S(2)}) copy-start(f32[1,1024,128]{2,0,1:T(1,128)S(1)} %fusion.95) | copy-start | bytes 1572868
  83.2 11.0 %collective-permute-start.1 = (f32[64,128]{1,0:T(8,128)S(1)}, f32[64,128]{1,0:T(8,128)S(1)}, u32[]{:S(2)}, u32[]{:S(2)}) collective-permute-start(f32[64,128]{1,0:T(8,128)S(1)} %get-tuple-element.7), channel_id=1, source_target_pairs={{0,32},{32,64},{64,96},{96,128},{128,160},{160,192},{192,224},{224... | collective-permute-start | bytes 98312 | tf_op jit(solution)/shard_map/ppermute | solution.py:28
  85.1 9.1 %collective-permute-start.2 = (f32[64,128]{1,0:T(8,128)S(1)}, f32[64,128]{1,0:T(8,128)S(1)}, u32[]{:S(2)}, u32[]{:S(2)}) collective-permute-start(f32[64,128]{1,0:T(8,128)S(1)} %get-tuple-element.8), channel_id=1, source_target_pairs={{32,0},{64,32},{96,64},{128,96},{160,128},{192,160},{224,192},{256... | collective-permute-start | bytes 98312 | tf_op jit(solution)/shard_map/ppermute | solution.py:29
  114.8 3.2 %copy-start.10 = (f32[1,256,1024]{2,1,0:T(8,128)S(1)}, f32[1,256,1024]{2,1,0:T(8,128)}, u32[]{:S(2)}) copy-start(f32[1,256,1024]{2,1,0:T(8,128)} %get-tuple-element.21) | copy-start | bytes 3145732
  114.8 3.2 %copy-start.11 = (f32[1,256,1024]{2,1,0:T(8,128)S(1)}, f32[1,256,1024]{2,1,0:T(8,128)}, u32[]{:S(2)}) copy-start(f32[1,256,1024]{2,1,0:T(8,128)} %get-tuple-element.22) | copy-start | bytes 3145732
  116.2 3.1 %copy-start.8 = (f32[1,256,1024]{2,1,0:T(8,128)S(1)}, f32[1,256,1024]{2,1,0:T(8,128)}, u32[]{:S(2)}) copy-start(f32[1,256,1024]{2,1,0:T(8,128)} %get-tuple-element.23) | copy-start | bytes 3145732
  116.2 3.1 %copy-start.9 = (f32[1,256,1024]{2,1,0:T(8,128)S(1)}, f32[1,256,1024]{2,1,0:T(8,128)}, u32[]{:S(2)}) copy-start(f32[1,256,1024]{2,1,0:T(8,128)} %get-tuple-element.24) | copy-start | bytes 3145732
  118.0 2.7 %copy-start.7 = (f32[1,256,1024]{2,1,0:T(8,128)S(1)}, f32[1,256,1024]{2,1,0:T(8,128)}, u32[]{:S(2)}) copy-start(f32[1,256,1024]{2,1,0:T(8,128)} %get-tuple-element.26) | copy-start | bytes 3145732
  239.5 1.2 copy-start.5
  239.5 1.5 copy-start.6
  241.1 3.6 %copy-start.3 = (f32[1,256,1024]{2,1,0:T(8,128)S(1)}, f32[1,256,1024]{2,1,0:T(8,128)}, u32[]{:S(2)}) copy-start(f32[1,256,1024]{2,1,0:T(8,128)} %get-tuple-element.16) | copy-start | bytes 3145732
  241.1 3.6 %copy-start.4 = (f32[1,256,1024]{2,1,0:T(8,128)S(1)}, f32[1,256,1024]{2,1,0:T(8,128)}, u32[]{:S(2)}) copy-start(f32[1,256,1024]{2,1,0:T(8,128)} %get-tuple-element.17) | copy-start | bytes 3145732
  244.7 3.6 %copy-start.1 = (f32[1,256,1024]{2,1,0:T(8,128)S(1)}, f32[1,256,1024]{2,1,0:T(8,128)}, u32[]{:S(2)}) copy-start(f32[1,256,1024]{2,1,0:T(8,128)} %get-tuple-element.15) | copy-start | bytes 3145732
  244.7 3.6 %copy-start.2 = (f32[1,256,1024]{2,1,0:T(8,128)S(1)}, f32[1,256,1024]{2,1,0:T(8,128)}, u32[]{:S(2)}) copy-start(f32[1,256,1024]{2,1,0:T(8,128)} %get-tuple-element.20) | copy-start | bytes 3145732
  248.3 3.6 %copy-start.12 = (f32[1,256,1024]{2,1,0:T(8,128)S(1)}, f32[1,256,1024]{2,1,0:T(8,128)}, u32[]{:S(2)}) copy-start(f32[1,256,1024]{2,1,0:T(8,128)} %get-tuple-element.9) | copy-start | bytes 3145732
  248.3 3.6 %copy-start.13 = (f32[1,256,1024]{2,1,0:T(8,128)S(1)}, f32[1,256,1024]{2,1,0:T(8,128)}, u32[]{:S(2)}) copy-start(f32[1,256,1024]{2,1,0:T(8,128)} %get-tuple-element.10) | copy-start | bytes 3145732
